TPU v7x, 32 devices: a whole 2x2x4 slice. The times are simulated.
32 devices in a mesh: tile: 8 (over y, x, core), depth: 4 (over z).
Axes of the slice: x: 2, y: 2, z: 4, core: 2. Of those that a mesh axis runs over, the one named last changes fastest.
Arguments:
- patches: float32 [512, 256, 256], P('tile', 'depth'), may hold values from -6 to 6
- patch_owner: int32 [512, 1], P('tile'), may hold values from 0 to 7; in each aligned block of 64 rows (0 to 63, 64 to 127, ...) at most 8 rows name the same one
- patch_level: int32 [512], P('tile'), may hold values from 0 to 63
- phases: float32 [512, 256, 256], P('tile', None, 'depth'), may hold values from -3.140625 to 3.140625
Outputs:
- intensity: float32 [512, 256, 256], P('tile', 'depth')
Inputs may be any that keep to these rules, and one draw needn't show every extreme that they name: `patch_owner`: among the 64 patches of one index of tile, at most 8 have the same owner.
All inputs are finite; a program needn't handle non-finite values.
Results may differ from a plain program's by a relative error of at most 0.00017.
Values sent between devices are 32-bit elements; how exact they have to be, the bound alone decides.
No kernel may reach another device: no remote copies, remote signals or barrier semaphores. Data moves between devices by JAX's collectives and lax.ppermute only.
A program may use at most 128 MiB of HBM per device.

v0:
```python
import math
import jax
import jax.numpy as jnp
from jax import lax
from jax.sharding import PartitionSpec as P

CAP = 8
HIGHEST_PRECISION = lax.Precision.HIGHEST


def tables(extent):
    indices = jnp.arange(extent, dtype=jnp.int32)
    product = indices[:, None] * indices[None, :] % extent
    angles = product.astype(jnp.float32) * (2.0 * math.pi / extent)
    return (jnp.cos(angles), jnp.sin(angles))


def right_apply(values, matrix):
    return jnp.einsum(
        "src,ck->srk",
        values,
        matrix,
        precision=HIGHEST_PRECISION,
        preferred_element_type=jnp.float32,
    )


def apply_rows(matrix, values):
    return jnp.einsum(
        "jk,skc->sjc",
        matrix,
        values,
        precision=HIGHEST_PRECISION,
        preferred_element_type=jnp.float32,
    )


def refocus_local(field, phase):
    extent = field.shape[2]
    cosine_table, sine_table = tables(extent)
    real_gain = jnp.cos(phase)
    imag_gain = jnp.sin(phase)
    col_real = right_apply(field, cosine_table)
    col_imag = -right_apply(field, sine_table)
    spec_real = apply_rows(cosine_table, col_real) + apply_rows(sine_table, col_imag)
    spec_imag = apply_rows(cosine_table, col_imag) - apply_rows(sine_table, col_real)
    prop_real = spec_real * real_gain - spec_imag * imag_gain
    prop_imag = spec_real * imag_gain + spec_imag * real_gain
    back_real = apply_rows(cosine_table, prop_real) - apply_rows(sine_table, prop_imag)
    back_imag = apply_rows(cosine_table, prop_imag) + apply_rows(sine_table, prop_real)
    field_real = right_apply(back_real, cosine_table) - right_apply(back_imag, sine_table)
    field_imag = right_apply(back_real, sine_table) + right_apply(back_imag, cosine_table)
    return (field_real * field_real + field_imag * field_imag) * (1.0 / float(extent) ** 4)


def on_device(patches, patch_owner, patch_level, phases):
    patch_count, row_count, extent = patches.shape
    levels = phases.shape[0]
    owners = lax.axis_size("tile")
    owner_column = patch_owner[:, 0]
    level_hot = (patch_level[:, None] == jnp.arange(levels, dtype=jnp.int32)[None, :]).astype(
        jnp.float32
    )
    owner_hot = (owner_column[:, None] == jnp.arange(owners, dtype=jnp.int32)[None, :]).astype(
        jnp.float32
    )
    before = jnp.tril(jnp.ones((patch_count, patch_count), jnp.float32), -1)
    rank_value = jnp.sum(
        jnp.dot(before, owner_hot, precision=HIGHEST_PRECISION, preferred_element_type=jnp.float32)
        * owner_hot,
        axis=1,
    )
    slot_index = owner_column * CAP + rank_value.astype(jnp.int32)
    slot_count = owners * CAP
    slot_hot = (jnp.arange(slot_count, dtype=jnp.int32)[:, None] == slot_index[None, :]).astype(
        jnp.float32
    )
    outgoing = jnp.dot(
        slot_hot,
        patches.reshape(patch_count, -1),
        precision=HIGHEST_PRECISION,
        preferred_element_type=jnp.float32,
    )
    outgoing = outgoing.reshape(slot_count, row_count, extent)
    chosen = jnp.dot(
        slot_hot, level_hot, precision=HIGHEST_PRECISION, preferred_element_type=jnp.float32
    )
    incoming, picked = (
        lax.all_to_all(outgoing, "tile", split_axis=0, concat_axis=0, tiled=True),
        lax.all_to_all(chosen, "tile", split_axis=0, concat_axis=0, tiled=True),
    )
    flattened = phases.reshape(levels, -1)
    phase_rows = jnp.dot(
        picked, flattened, precision=HIGHEST_PRECISION, preferred_element_type=jnp.float32
    )
    phase_rows = phase_rows.reshape(slot_count, phases.shape[1], phases.shape[2])
    phase_turned = jnp.transpose(phase_rows, (0, 2, 1))
    whole_field, whole_phase = (
        lax.all_to_all(incoming, "depth", split_axis=0, concat_axis=1, tiled=True),
        lax.all_to_all(phase_turned, "depth", split_axis=0, concat_axis=1, tiled=True),
    )
    local_result = refocus_local(whole_field, jnp.transpose(whole_phase, (0, 2, 1)))
    result = lax.all_to_all(local_result, "depth", split_axis=1, concat_axis=0, tiled=True)
    returned = lax.all_to_all(result, "tile", split_axis=0, concat_axis=0, tiled=True)
    placed = jnp.dot(
        slot_hot.T,
        returned.reshape(slot_count, -1),
        precision=HIGHEST_PRECISION,
        preferred_element_type=jnp.float32,
    )
    return placed.reshape(patch_count, row_count, extent)


def solution(mesh):
    return jax.shard_map(
        on_device,
        mesh=mesh,
        in_specs=(P("tile", "depth", None), P("tile", None), P("tile"), P("tile", None, "depth")),
        out_specs=P("tile", "depth", None),
        check_vma=False,
    )
```

profile of v0, /device:TPU:0, one launch (start us, length us, event | category | flops | bytes accessed | tf_op | source)
XLA Modules:
  0.0 528.9 jit_solution(16689904573134012535)
XLA Ops:
  0.0 0.9 fusion.42
  1.0 0.7 convert_add_fusion
  1.6 0.9 convolution_bitcast_fusion.1
  2.6 0.7 reshape.39
  3.2 5.2 all-to-all-start.2
  8.4 6.9 %fusion.3 = f32[64,64,256]{2,0,1:T(8,128)S(1)} fusion(s32[64]{0:T(128)S(1)} %convert_add_fusion, f32[8,8,64,256]{3,2,1,0:T(8,128)} %bitcast.140), kind=kOutput, calls=%fused_computation.3 | convolution fusion | flops 805310464 | bytes 8388864 | tf_op jit(solution)/shard_map/dot_general | solution.py:78
  15.3 4.4 copy.58
  19.7 0.0 all-to-all-done.2
  19.7 4.8 all-to-all-start
  24.5 6.9 %copy.62 = f32[64,256,64]{2,1,0:T(8,128)} copy(f32[64,256,64]{1,2,0:T(8,128)} %param.7) | data formatting | bytes 8388608 | tf_op args[3]
  31.4 6.9 %reshape.32 = f32[64,16384]{1,0:T(8,128)} reshape(f32[64,256,64]{2,1,0:T(8,128)} %copy.62) | data formatting | bytes 8388608 | tf_op jit(solution)/shard_map/reshape | solution.py:92
  38.3 7.4 %dot_general.79 = f32[256,64,64]{1,0,2:T(8,128)} reshape(f32[16384,64]{0,1:T(8,128)} %bitcast.134) | data formatting | bytes 8388608 | tf_op jit(solution)/shard_map/dot_general | solution.py:93
  45.6 7.3 %copy.63 = f32[256,64,64]{0,2,1:T(8,128)} copy(f32[256,64,64]{1,0,2:T(8,128)} %dot_general.79) | data formatting | bytes 8388608 | tf_op jit(solution)/shard_map/dot_general | solution.py:93
  52.9 0.5 broadcast.68
  53.5 0.6 reduce
  54.1 0.1 reshape.40
  54.2 5.5 %convolution_bitcast_fusion = f32[64,64,256]{2,0,1:T(8,128)S(1)} fusion(f32[256,64,64]{0,2,1:T(8,128)} %copy.63, f32[8,8,64]{2,1,0:T(8,128)S(1)} %reshape.40), kind=kOutput, calls=%fused_computation.33 | convolution fusion | flops 805306368 | bytes 8404992 | tf_op jit(solution)/shard_map/dot_general | solution.py:93
  59.7 4.4 copy.64
  64.1 9.5 %all-to-all-done = f32[64,64,256]{2,1,0:T(8,128)} async-done(((f32[64,64,256]{2,1,0:T(8,128)}), f32[64,64,256]{2,1,0:T(8,128)}, u32[]{:S(2)}, u32[]{:S(2)}) %all-to-all-start) | async-done | bytes 4194336 | tf_op jit(solution)/shard_map/all_to_all | solution.py:89
  73.6 96.2 %all_to_all.67 = f32[64,64,256]{2,1,0:T(8,128)} all-to-all(f32[64,64,256]{2,1,0:T(8,128)} %copy.64), channel_id=1, replica_groups=mesh['tile'=8,'depth'=4] {'depth'}, dimensions={0} | all-to-all | bytes 8388608 | tf_op jit(solution)/shard_map/all_to_all | solution.py:100
  169.8 4.8 all-to-all-start.1
  174.7 16.0 %fusion.154 = (f32[64,64,256]{2,1,0:T(8,128)S(1)}, f32[64,64,256]{2,1,0:T(8,128)S(1)}) fusion(f32[64,64,256]{2,1,0:T(8,128)} %all_to_all.67), kind=kLoop, calls=%fused_computation.145 | loop fusion | bytes 12582912 | tf_op jit(solution)/shard_map/sin | solution.py:42
  190.6 2.3 copy.65
  192.9 2.3 copy.68
  195.2 71.0 %all-to-all-done.1 = f32[64,64,256]{2,1,0:T(8,128)} async-done(((f32[64,64,256]{2,1,0:T(8,128)}), f32[64,64,256]{2,1,0:T(8,128)}, u32[]{:S(2)}, u32[]{:S(2)}) %all-to-all-start.1) | async-done | bytes 4194336 | tf_op jit(solution)/shard_map/all_to_all | solution.py:99
  266.2 2.5 copy.59
  268.7 5.2 fusion.62
  273.9 4.6 fusion.53
  278.4 5.0 fusion.50
  283.5 6.9 %fusion.60 = f32[16,256,256]{2,1,0:T(8,128)} fusion(f32[16,256,256]{1,2,0:T(8,128)S(1)} %fusion.62), kind=kOutput, calls=%fused_computation.61 | convolution fusion | flops 3222142976 | bytes 8388608 | tf_op jit(solution)/shard_map/jk,skc->sjc/dot_general | solution.py:29
  290.4 0.0 copy-start
  290.4 8.2 %fusion.31 = f32[16,256,256]{2,1,0:T(8,128)S(1)} fusion(f32[16,256,256]{2,1,0:T(8,128)S(1)} %fusion.50, f32[16,256,256]{2,1,0:T(8,128)S(1)} %fusion.53), kind=kOutput, calls=%fused_computation.35 | convolution fusion | flops 3224240128 | bytes 12582912 | tf_op jit(solution)/shard_map/jk,skc->sjc/dot_general | solution.py:29
  298.6 0.0 copy-done
  298.6 13.1 %fusion.18 = (f32[16,256,256]{2,1,0:T(8,128)S(1)}, f32[16,256,256]{2,1,0:T(8,128)S(1)}) fusion(f32[4,16,64,256]{3,2,0,1:T(8,128)S(1)} %copy-done, f32[16,256,256]{2,1,0:T(8,128)S(1)} %fusion.31, f32[4,16,64,256]{3,2,0,1:T(8,128)} %copy.68, f32[16,256,256]{2,1,0:T(8,128)} %fusion.60, f32[16,256,256]{2,1,0:T(8,128)S(1)} %fusion.53), kind=kOutput, calls=%fused_computation.20 | convolution fusion | flops 3230531584 | bytes 29360128 | tf_op jit(solution)/shard_map/jk,skc->sjc/dot_general | solution.py:29
  311.7 4.8 fusion.16
  316.5 4.4 fusion.14
  320.9 4.4 fusion.37
  325.3 8.4 %fusion.6 = f32[16,256,256]{2,1,0:T(8,128)S(1)} fusion(f32[16,256,256]{2,1,0:T(8,128)S(1)} %fusion.37), kind=kOutput, calls=%fused_computation.6 | convolution fusion | flops 3222142976 | bytes 8388608 | tf_op jit(solution)/shard_map/src,ck->srk/dot_general | solution.py:19
  333.7 8.2 %fusion.8 = f32[16,256,256]{2,1,0:T(8,128)S(1)} fusion(f32[16,256,256]{2,1,0:T(8,128)S(1)} %fusion.37), kind=kOutput, calls=%fused_computation.8 | convolution fusion | flops 3222142976 | bytes 8388608 | tf_op jit(solution)/shard_map/src,ck->srk/dot_general | solution.py:19
  342.0 4.8 fusion.34
  346.7 8.3 %fusion.10 = f32[16,256,256]{2,1,0:T(8,128)S(1)} fusion(f32[16,256,256]{2,1,0:T(8,128)S(1)} %fusion.34), kind=kOutput, calls=%fused_computation.10 | convolution fusion | flops 3222142976 | bytes 8388608 | tf_op jit(solution)/shard_map/src,ck->srk/dot_general | solution.py:19
  355.0 8.8 %add_multiply_fusion = f32[16,256,256]{2,1,0:T(8,128)S(1)} fusion(f32[16,256,256]{2,1,0:T(8,128)S(1)} %fusion.10, f32[16,256,256]{2,1,0:T(8,128)S(1)} %fusion.6, f32[16,256,256]{2,1,0:T(8,128)S(1)} %fusion.8, f32[16,256,256]{2,1,0:T(8,128)S(1)} %fusion.34), kind=kOutput, calls=%fused_computation.28 | convolution fusion | flops 3228434432 | bytes 20971520 | tf_op jit(solution)/shard_map/src,ck->srk/dot_general | solution.py:19
  363.8 2.7 copy.73
  366.5 95.3 %all_to_all.68 = f32[16,256,256]{2,0,1:T(8,128)S(1)} all-to-all(f32[16,256,256]{2,0,1:T(8,128)S(1)} %copy.73), channel_id=1, replica_groups=mesh['tile'=8,'depth'=4] {'depth'}, dimensions={1} | all-to-all | bytes 8388608 | tf_op jit(solution)/shard_map/all_to_all | solution.py:103
  461.8 2.4 copy.75
  464.2 55.0 %all_to_all.69 = f32[64,64,256]{2,1,0:T(8,128)S(1)} all-to-all(f32[64,64,256]{2,1,0:T(8,128)S(1)} %bitcast.139), channel_id=1, replica_groups=mesh['tile'=8,'depth'=4] {'tile'}, dimensions={0} | all-to-all | bytes 8388608 | tf_op jit(solution)/shard_map/all_to_all | solution.py:104
  519.2 4.8 fusion
  524.0 4.4 copy.77
  (1 shorter events, 0.0 us)
Async XLA Ops:
  3.2 16.5 %all-to-all-start.2 = ((f32[8,1,512]{2,1,0:T(1,128)}), f32[8,1,512]{2,1,0:T(1,128)S(1)}, u32[]{:S(2)}, u32[]{:S(2)}) async-start(f32[8,1,512]{2,1,0:T(1,128)} %reshape.39), calls=%async_computation.2 | async-start | bytes 32768 | tf_op jit(solution)/shard_map/all_to_all | solution.py:90
  19.7 53.9 %all-to-all-start = ((f32[64,64,256]{2,1,0:T(8,128)}), f32[64,64,256]{2,1,0:T(8,128)}, u32[]{:S(2)}, u32[]{:S(2)}) async-start(f32[64,64,256]{2,1,0:T(8,128)} %copy.58), calls=%async_computation | async-start | bytes 8388608 | tf_op jit(solution)/shard_map/all_to_all | solution.py:89
  169.8 96.4 %all-to-all-start.1 = ((f32[64,64,256]{2,1,0:T(8,128)}), f32[64,64,256]{2,1,0:T(8,128)}, u32[]{:S(2)}, u32[]{:S(2)}) async-start(f32[64,64,256]{2,1,0:T(8,128)} %all-to-all-done), calls=%async_computation.1 | async-start | bytes 8388608 | tf_op jit(solution)/shard_map/all_to_all | solution.py:99
  290.4 8.2 %copy-start = (f32[4,16,64,256]{3,2,0,1:T(8,128)S(1)}, f32[4,16,64,256]{3,2,0,1:T(8,128)}, u32[]{:S(2)}) copy-start(f32[4,16,64,256]{3,2,0,1:T(8,128)} %copy.65) | copy-start | bytes 12582916
where the time goes:
time: 535 us; the launch traced here: 529 us
  blocking collectives  246 us (46%)
  matrix products  114 us (21%)
  waiting for transfers between devices  80.5 us (15%)
  local copies, waits for them, and re-layouts  71.1 us (13%)
  starting transfers between devices  14.8 us (3%)
    all_to_all x1, blocking collectives, on_device(): lax.all_to_all(phase_turned, 'depth', split_axis=0, concat_axis=1, tiled=...  96.2 us
    all_to_all x1, blocking collectives, on_device(): lax.all_to_all(local_result, 'depth', split_axis=1, concat_axis=0, tiled=...  95.3 us
    all_to_all x1, waiting for transfers between devices, on_device(): lax.all_to_all(incoming, 'depth', split_axis=0, concat_axis=1, tiled=True)  71 us
    all_to_all x1, blocking collectives, on_device(): lax.all_to_all(result, 'tile', split_axis=0, concat_axis=0, tiled=True)  55 us
    dot_general x8, matrix products, apply_rows(): jnp.einsum('jk,skc->sjc', matrix, values, precision=HIGHEST_PRECISION, pr...  51.6 us
    dot_general x6, matrix products, right_apply(): jnp.einsum('src,ck->srk', values, matrix, precision=HIGHEST_PRECISION, pr...  43.4 us
    sin x2, local copies, waits for them, and re-layouts, refocus_local(): imag_gain = jnp.sin(phase)  18.2 us
    dot_general x2, local copies, waits for them, and re-layouts, on_device(): jnp.dot(picked, flattened, precision=HIGHEST_PRECISION, preferred_element...  14.7 us
  transfers between devices with their start and end apart: 3, of which 2 were waited for; matrix products, arithmetic and copies ran while one was open for 13% of the time, Pallas kernels for 0%

commit v1 on v0

--- a/solution.py
+++ b/solution.py
@@ -6,6 +6,23 @@
 
 CAP = 8
 HIGHEST_PRECISION = lax.Precision.HIGHEST
+
+
+def post_digits(inp):
+    lane_axis = "depth"
+    outcome_arr, then = (lax.axis_size(lane_axis), lax.axis_index(lane_axis))
+    prior = inp.shape[0] // outcome_arr
+    x_now = list(inp.shape)
+    x_now[0] = prior
+    local_next = x_now[1]
+    x_now[1] = local_next * outcome_arr
+    odd = jnp.zeros(x_now, inp.dtype)
+    for h in range(outcome_arr):
+        y = lax.dynamic_slice_in_dim(inp, (then ^ h) * prior, prior, axis=0)
+        if h:
+            y = lax.ppermute(y, lane_axis, list(map(lambda kk: (kk, kk ^ h), range(outcome_arr))))
+        odd = lax.dynamic_update_slice_in_dim(odd, y, (then ^ h) * local_next, axis=1)
+    return odd
 
 
 def tables(extent):
@@ -96,7 +113,7 @@
     phase_rows = phase_rows.reshape(slot_count, phases.shape[1], phases.shape[2])
     phase_turned = jnp.transpose(phase_rows, (0, 2, 1))
     whole_field, whole_phase = (
-        lax.all_to_all(incoming, "depth", split_axis=0, concat_axis=1, tiled=True),
+        post_digits(incoming),
         lax.all_to_all(phase_turned, "depth", split_axis=0, concat_axis=1, tiled=True),
     )
     local_result = refocus_local(whole_field, jnp.transpose(whole_phase, (0, 2, 1)))

time: 535 us -> 556 us (1.039)
  blocking collectives: 246 us -> 167 us
  waiting for transfers between devices: 80.5 us -> 156 us
  local copies, waits for them, and re-layouts: 71.1 us -> 84.9 us
  matrix products: 114 us -> 120 us
    ppermute x0 -> x3, waiting for transfers between devices: none -> 146 us  [post_digits(): lax.ppermute(y, lane_axis, list(map(lambda kk: (kk, kk ^ h), range(outcom...]
    all_to_all x1 -> x0, blocking collectives: 96.2 us -> none  [on_device(): lax.all_to_all(phase_turned, 'depth', split_axis=0, concat_axis=1, tiled=...]
    all_to_all x1, waiting for transfers between devices: 71 us -> 0.01 us  [on_device(): lax.all_to_all(phase_turned, 'depth', split_axis=0, concat_axis=1, tiled=...]
    all_to_all x1, blocking collectives: 95.3 us -> 113 us  [on_device(): lax.all_to_all(local_result, 'depth', split_axis=1, concat_axis=0, tiled=...]
    dynamic_update_slice x0 -> x3, local copies, waits for them, and re-layouts: none -> 6.99 us  [post_digits(): lax.dynamic_update_slice_in_dim(odd, y, (then ^ h) * local_next, axis=1)]
  transfers between devices with their start and end apart: 3 -> 6, of which waited for: 2 -> 3; matrix products, arithmetic and copies ran while one was open for 13% -> 18% of each run, Pallas kernels for 0% -> 0%
where the time goes in v1:
time: 556 us; the launch traced here: 550 us
  blocking collectives  167 us (30%)
  waiting for transfers between devices  156 us (28%)
  matrix products  120 us (22%)
  local copies, waits for them, and re-layouts  84.9 us (15%)
  starting transfers between devices  19.5 us (4%)
    ppermute x3, waiting for transfers between devices, post_digits(): lax.ppermute(y, lane_axis, list(map(lambda kk: (kk, kk ^ h), range(outcom...  146 us
    all_to_all x1, blocking collectives, on_device(): lax.all_to_all(local_result, 'depth', split_axis=1, concat_axis=0, tiled=...  113 us
    all_to_all x1, blocking collectives, on_device(): lax.all_to_all(result, 'tile', split_axis=0, concat_axis=0, tiled=True)  53.9 us
    dot_general x8, matrix products, apply_rows(): jnp.einsum('jk,skc->sjc', matrix, values, precision=HIGHEST_PRECISION, pr...  52.9 us
    dot_general x6, matrix products, right_apply(): jnp.einsum('src,ck->srk', values, matrix, precision=HIGHEST_PRECISION, pr...  48.5 us
    sin x2, local copies, waits for them, and re-layouts, refocus_local(): imag_gain = jnp.sin(phase)  18.3 us
    dot_general x2, local copies, waits for them, and re-layouts, on_device(): jnp.dot(picked, flattened, precision=HIGHEST_PRECISION, preferred_element...  14.7 us
  transfers between devices with their start and end apart: 6, of which 3 were waited for; matrix products, arithmetic and copies ran while one was open for 18% of the time, Pallas kernels for 0%

profile of v1, /device:TPU:0, one launch (start us, length us, event | category | flops | bytes accessed | tf_op | source)
XLA Modules:
  0.0 549.6 jit_solution(16091366385730930499)
XLA Ops:
  0.0 0.9 fusion.42
  1.6 0.9 convolution_bitcast_fusion.1
  3.2 5.2 all-to-all-start.1
  8.4 6.9 %fusion.3 = f32[64,64,256]{2,0,1:T(8,128)S(1)} fusion(s32[64]{0:T(128)S(1)} %convert_add_fusion, f32[8,8,64,256]{3,2,1,0:T(8,128)} %bitcast.134), kind=kOutput, calls=%fused_computation.3 | convolution fusion | flops 805310464 | bytes 8388864 | tf_op jit(solution)/shard_map/dot_general | solution.py:95
  15.3 4.4 copy.63
  19.7 4.8 all-to-all-start
  24.5 6.9 %copy.66 = f32[64,256,64]{2,1,0:T(8,128)} copy(f32[64,256,64]{1,2,0:T(8,128)} %param.7) | data formatting | bytes 8388608 | tf_op args[3]
  31.4 6.9 %reshape.32 = f32[64,16384]{1,0:T(8,128)} reshape(f32[64,256,64]{2,1,0:T(8,128)} %copy.66) | data formatting | bytes 8388608 | tf_op jit(solution)/shard_map/reshape | solution.py:109
  38.3 7.4 %dot_general.79 = f32[256,64,64]{1,0,2:T(8,128)} reshape(f32[16384,64]{0,1:T(8,128)} %bitcast.128) | data formatting | bytes 8388608 | tf_op jit(solution)/shard_map/dot_general | solution.py:110
  45.7 7.3 %copy.67 = f32[256,64,64]{0,2,1:T(8,128)} copy(f32[256,64,64]{1,0,2:T(8,128)} %dot_general.79) | data formatting | bytes 8388608 | tf_op jit(solution)/shard_map/dot_general | solution.py:110
  54.2 5.5 convolution_bitcast_fusion
  59.7 4.4 copy.68
  64.2 9.5 %all-to-all-done = f32[64,64,256]{2,1,0:T(8,128)} async-done(((f32[64,64,256]{2,1,0:T(8,128)}), f32[64,64,256]{2,1,0:T(8,128)}, u32[]{:S(2)}, u32[]{:S(2)}) %all-to-all-start) | async-done | bytes 4194336 | tf_op jit(solution)/shard_map/all_to_all | solution.py:106
  73.6 5.1 all-to-all-start.2
  78.8 2.4 broadcast_in_dim.10
  81.2 3.6 constant_dynamic-slice_fusion
  84.8 2.0 collective-permute-start
  86.8 2.3 collective-permute-start.1
  89.2 80.7 %collective-permute-done = f32[16,64,256]{2,1,0:T(8,128)} collective-permute-done((f32[16,64,256]{2,1,0:T(8,128)S(1)}, f32[16,64,256]{2,1,0:T(8,128)}, u32[]{:S(2)}, u32[]{:S(2)}) %collective-permute-start) | collective-permute-done | bytes 1048608 | tf_op jit(solution)/shard_map/ppermute | solution.py:23
  169.9 2.3 constant_dynamic-update-slice_fusion.2
  172.3 65.5 %collective-permute-done.1 = f32[16,64,256]{2,1,0:T(8,128)} collective-permute-done((f32[16,64,256]{2,1,0:T(8,128)S(1)}, f32[16,64,256]{2,1,0:T(8,128)}, u32[]{:S(2)}, u32[]{:S(2)}) %collective-permute-start.1) | collective-permute-done | bytes 1048608 | tf_op jit(solution)/shard_map/ppermute | solution.py:23
  237.8 2.4 constant_dynamic-update-slice_fusion.1
  240.2 2.3 constant_dynamic-update-slice_fusion
  242.5 7.6 %fusion.62 = f32[16,256,256]{1,2,0:T(8,128)S(1)} fusion(f32[16,256,256]{2,1,0:T(8,128)} %constant_dynamic-update-slice_fusion), kind=kOutput, calls=%fused_computation.64 | convolution fusion | flops 3222142976 | bytes 8388608 | tf_op jit(solution)/shard_map/src,ck->srk/dot_general | solution.py:36
  250.1 7.2 %fusion.53 = f32[16,256,256]{2,1,0:T(8,128)S(1)} fusion(f32[16,256,256]{2,1,0:T(8,128)} %constant_dynamic-update-slice_fusion), kind=kOutput, calls=%fused_computation.55 | convolution fusion | flops 3222142976 | bytes 8388608 | tf_op jit(solution)/shard_map/src,ck->srk/dot_general | solution.py:36
  257.3 4.4 fusion.50
  261.7 7.4 %fusion.60 = f32[16,256,256]{2,1,0:T(8,128)} fusion(f32[16,256,256]{1,2,0:T(8,128)S(1)} %fusion.62), kind=kOutput, calls=%fused_computation.62 | convolution fusion | flops 3222142976 | bytes 8388608 | tf_op jit(solution)/shard_map/jk,skc->sjc/dot_general | solution.py:46
  269.1 10.0 %fusion.31 = f32[16,256,256]{2,1,0:T(8,128)} fusion(f32[16,256,256]{2,1,0:T(8,128)S(1)} %fusion.50, f32[16,256,256]{2,1,0:T(8,128)S(1)} %fusion.53), kind=kOutput, calls=%fused_computation.35 | convolution fusion | flops 3224240128 | bytes 12582912 | tf_op jit(solution)/shard_map/jk,skc->sjc/dot_general | solution.py:46
  279.2 15.9 %fusion.154 = (f32[64,64,256]{2,1,0:T(8,128)S(1)}, f32[64,64,256]{2,1,0:T(8,128)S(1)}) fusion(f32[64,64,256]{2,1,0:T(8,128)} %all-to-all-done.2), kind=kLoop, calls=%fused_computation.152 | loop fusion | bytes 12582912 | tf_op jit(solution)/shard_map/sin | solution.py:59
  295.1 2.4 copy.69
  297.5 2.4 copy.72
  299.9 1.9 copy-done.1
  301.8 1.2 copy-done.2
  303.0 12.6 %fusion.18 = (f32[16,256,256]{2,1,0:T(8,128)S(1)}, f32[16,256,256]{2,1,0:T(8,128)S(1)}) fusion(f32[4,16,64,256]{3,2,0,1:T(8,128)} %copy.69, f32[16,256,256]{2,1,0:T(8,128)S(1)} %copy-done.2, f32[4,16,64,256]{3,2,0,1:T(8,128)} %copy.72, f32[16,256,256]{2,1,0:T(8,128)S(1)} %copy-done.3, f32[16,256,256]{2,1,0:T(8,128)S(1)} %copy-done.1), kind=kOutput, calls=%fused_computation.20 | convolution fusion | flops 3230531584 | bytes 29360128 | tf_op jit(solution)/shard_map/jk,skc->sjc/dot_general | solution.py:46
  315.6 4.8 fusion.16
  320.4 4.4 fusion.14
  324.8 4.4 fusion.37
  329.3 8.4 %fusion.6 = f32[16,256,256]{2,1,0:T(8,128)S(1)} fusion(f32[16,256,256]{2,1,0:T(8,128)S(1)} %fusion.37), kind=kOutput, calls=%fused_computation.6 | convolution fusion | flops 3222142976 | bytes 8388608 | tf_op jit(solution)/shard_map/src,ck->srk/dot_general | solution.py:36
  337.7 8.2 %fusion.8 = f32[16,256,256]{2,1,0:T(8,128)S(1)} fusion(f32[16,256,256]{2,1,0:T(8,128)S(1)} %fusion.37), kind=kOutput, calls=%fused_computation.8 | convolution fusion | flops 3222142976 | bytes 8388608 | tf_op jit(solution)/shard_map/src,ck->srk/dot_general | solution.py:36
  345.9 4.8 fusion.34
  350.7 8.3 %fusion.10 = f32[16,256,256]{2,1,0:T(8,128)S(1)} fusion(f32[16,256,256]{2,1,0:T(8,128)S(1)} %fusion.34), kind=kOutput, calls=%fused_computation.10 | convolution fusion | flops 3222142976 | bytes 8388608 | tf_op jit(solution)/shard_map/src,ck->srk/dot_general | solution.py:36
  359.0 8.8 %add_multiply_fusion = f32[16,256,256]{2,1,0:T(8,128)S(1)} fusion(f32[16,256,256]{2,1,0:T(8,128)S(1)} %fusion.10, f32[16,256,256]{2,1,0:T(8,128)S(1)} %fusion.6, f32[16,256,256]{2,1,0:T(8,128)S(1)} %fusion.8, f32[16,256,256]{2,1,0:T(8,128)S(1)} %fusion.34), kind=kOutput, calls=%fused_computation.28 | convolution fusion | flops 3228434432 | bytes 20971520 | tf_op jit(solution)/shard_map/src,ck->srk/dot_general | solution.py:36
  367.8 2.7 copy.77
  370.5 113.2 %all_to_all.49 = f32[16,256,256]{2,0,1:T(8,128)S(1)} all-to-all(f32[16,256,256]{2,0,1:T(8,128)S(1)} %copy.77), channel_id=1, replica_groups=mesh['tile'=8,'depth'=4] {'depth'}, dimensions={1} | all-to-all | bytes 8388608 | tf_op jit(solution)/shard_map/all_to_all | solution.py:120
  483.7 2.4 copy.79
  486.1 53.9 %all_to_all.50 = f32[64,64,256]{2,1,0:T(8,128)S(1)} all-to-all(f32[64,64,256]{2,1,0:T(8,128)S(1)} %bitcast.133), channel_id=1, replica_groups=mesh['tile'=8,'depth'=4] {'tile'}, dimensions={0} | all-to-all | bytes 8388608 | tf_op jit(solution)/shard_map/all_to_all | solution.py:121
  539.9 4.8 fusion
  544.7 4.4 copy.81
  (16 shorter events, 2.8 us)
Async XLA Ops:
  3.2 16.5 %all-to-all-start.1 = ((f32[8,1,512]{2,1,0:T(1,128)}), f32[8,1,512]{2,1,0:T(1,128)S(1)}, u32[]{:S(2)}, u32[]{:S(2)}) async-start(f32[8,1,512]{2,1,0:T(1,128)} %reshape.39), calls=%async_computation.1 | async-start | bytes 32768 | tf_op jit(solution)/shard_map/all_to_all | solution.py:107
  19.7 53.9 %all-to-all-start = ((f32[64,64,256]{2,1,0:T(8,128)}), f32[64,64,256]{2,1,0:T(8,128)}, u32[]{:S(2)}, u32[]{:S(2)}) async-start(f32[64,64,256]{2,1,0:T(8,128)} %copy.63), calls=%async_computation | async-start | bytes 8388608 | tf_op jit(solution)/shard_map/all_to_all | solution.py:106
  73.6 205.5 %all-to-all-start.2 = ((f32[64,64,256]{2,1,0:T(8,128)}), f32[64,64,256]{2,1,0:T(8,128)}, u32[]{:S(2)}, u32[]{:S(2)}) async-start(f32[64,64,256]{2,1,0:T(8,128)} %copy.68), calls=%async_computation.2 | async-start | bytes 8388608 | tf_op jit(solution)/shard_map/all_to_all | solution.py:117
  84.8 85.1 %collective-permute-start = (f32[16,64,256]{2,1,0:T(8,128)S(1)}, f32[16,64,256]{2,1,0:T(8,128)}, u32[]{:S(2)}, u32[]{:S(2)}) collective-permute-start(f32[16,64,256]{2,1,0:T(8,128)S(1)} %get-tuple-element.11), channel_id=1, source_target_pairs={{0,1},{1,0},{2,3},{3,2},{4,5},{5,4},{6,7},{7,6},{8,9},{9,8},{10,11... | collective-permute-start | bytes 3145736 | tf_op jit(solution)/shard_map/ppermute | solution.py:23
  86.8 151.0 %collective-permute-start.1 = (f32[16,64,256]{2,1,0:T(8,128)S(1)}, f32[16,64,256]{2,1,0:T(8,128)}, u32[]{:S(2)}, u32[]{:S(2)}) collective-permute-start(f32[16,64,256]{2,1,0:T(8,128)S(1)} %get-tuple-element.10), channel_id=1, source_target_pairs={{0,2},{1,3},{2,0},{3,1},{4,6},{5,7},{6,4},{7,5},{8,10},{9,11},{10,... | collective-permute-start | bytes 3145736 | tf_op jit(solution)/shard_map/ppermute | solution.py:23
  89.1 151.1 %collective-permute-start.2 = (f32[16,64,256]{2,1,0:T(8,128)S(1)}, f32[16,64,256]{2,1,0:T(8,128)}, u32[]{:S(2)}, u32[]{:S(2)}) collective-permute-start(f32[16,64,256]{2,1,0:T(8,128)S(1)} %get-tuple-element.9), channel_id=1, source_target_pairs={{0,3},{1,2},{2,1},{3,0},{4,7},{5,6},{6,5},{7,4},{8,11},{9,10},{10,... | collective-permute-start | bytes 3145736 | tf_op jit(solution)/shard_map/ppermute | solution.py:23
  257.3 11.8 %copy-start = (f32[16,256,256]{2,1,0:T(8,128)}, f32[16,256,256]{2,1,0:T(8,128)S(1)}, u32[]{:S(2)}) copy-start(f32[16,256,256]{2,1,0:T(8,128)S(1)} %fusion.53) | copy-start | bytes 12582916
  295.1 4.9 copy-start.3
  297.5 4.3 copy-start.1
  297.5 5.5 copy-start.2
